TPU v7x, 128 devices: a whole 4x4x4 slice. The times are simulated.
128 devices in a mesh: seq: 16 (over y, z), head: 8 (over x, core).
Axes of the slice: x: 4, y: 4, z: 4, core: 2. Of those that a mesh axis runs over, the one named last changes fastest.
Arguments:
- qkv: bfloat16 [12288, 3, 3072], P(('seq', 'head')), may hold values from -21 to 21, as said below
- window_tiles: int32 [32, 27], replicated, may hold values from -1 to 31, as said below
Outputs:
- attended: bfloat16 [12288, 3072], P(('seq', 'head'))
Inputs may be any that keep to these rules, and one draw needn't show every extreme that they name: `window_tiles`: row a lists distinct tile ids or -1; its first entry is a itself; every other id is of a tile that differs from tile a by at most one tile in time, in height and in width. `qkv`: entries are finite.
All inputs are finite; a program needn't handle non-finite values.
Results may differ from a plain program's by a relative error of at most 0.012.
Values may be sent and summed in bfloat16 or wider, within the bound.
A program may use at most 128 MiB of HBM per device.

v0:
```python
import jax
import jax.numpy as jnp
from jax import lax
from jax.sharding import PartitionSpec as P

HDIM = 128
TF = 6
TH = 8
TW = 8
HT = 4


def passed_along(value, axis, steps):
    count = lax.axis_size(axis)
    pairs = [(source, (source + steps) % count) for source in range(count)]
    return lax.ppermute(value, axis, pairs)


def shortened(value):

    def short(part):
        return part.astype(jnp.bfloat16) if part.dtype == jnp.float32 else part

    return jax.tree.map(short, value)


def band_count(line, band):
    return line // (TH * HT) * TH + jnp.clip(line % (TH * HT) - band * TH, 0, TH)


def band_line(count, band):
    return count // TH * (TH * HT) + band * TH + count % TH


def capacity(block):
    return block // (TH * HT) * TH + min(block % (TH * HT), TH)


def pack_lines(block_rows, start, block, cap):
    bands = jnp.arange(HT, dtype=jnp.int32)[:, None]
    slots = jnp.arange(cap, dtype=jnp.int32)[None, :]
    line = band_line(band_count(start, bands) + slots, bands)
    valid = line < start + block
    picked = block_rows[jnp.where(valid, line - start, 0)]
    valid = valid.reshape(valid.shape + (1,) * (picked.ndim - 2))
    return jnp.where(valid, picked, jnp.zeros((), picked.dtype))


def unpack_lines(received, block, cap, band, total_lines):
    count = jnp.arange(total_lines, dtype=jnp.int32)
    line = band_line(count, band)
    source = line // block
    slot = count - band_count(source * block, band)
    flat = received.reshape((-1,) + received.shape[2:])
    return flat[source * cap + slot]


def pack_back(band_out, block, cap, band, targets):
    dests = jnp.arange(targets, dtype=jnp.int32)[:, None]
    slots = jnp.arange(cap, dtype=jnp.int32)[None, :]
    count = band_count(dests * block, band) + slots
    valid = band_line(count, band) < (dests + 1) * block
    picked = band_out[jnp.where(valid, count, 0)]
    return jnp.where(valid[:, :, None, None], picked, jnp.zeros((), picked.dtype))


def head_attend(query, keys, values, usable_rows, scale):
    scores = (
        lax.dot_general(query, keys, (((1,), (1,)), ((), ())), preferred_element_type=jnp.float32)
        * scale
    )
    scores = jnp.where(usable_rows[None, :], scores, -1e30)
    peak = jnp.max(scores, axis=1, keepdims=True)
    expo = jnp.exp(scores - peak)
    weights = (expo / jnp.sum(expo, axis=1, keepdims=True)).astype(jnp.bfloat16)
    return jnp.dot(weights, values, preferred_element_type=jnp.float32).astype(jnp.bfloat16)


def body(qkv, window_tiles):
    seq_count = lax.axis_size("seq")
    head_count = lax.axis_size("head")
    rows = qkv.shape[0]
    width = qkv.shape[2]
    group_width = width // head_count
    head_local = group_width // HDIM
    tile_size = TF * TH * TW
    col_tiles = seq_count // HT
    rotation = col_tiles // 2
    line_width = TW * col_tiles
    lines = rows // line_width
    own_tiles = window_tiles.shape[0] // seq_count
    slot_count = window_tiles.shape[1]
    total_lines = own_tiles * TF * TH
    seq_index = lax.axis_index("seq")
    head_index = lax.axis_index("head")
    my_block = (seq_index + rotation) % seq_count
    my_band = my_block // col_tiles
    my_col = my_block % col_tiles
    my_window = lax.dynamic_slice_in_dim(window_tiles, my_block * own_tiles, own_tiles, 0)
    cap = capacity(lines)
    start = (seq_index * head_count + head_index) * lines
    packed = pack_lines(qkv.reshape(lines, line_width, 3, width), start, lines, cap)
    packed = packed.reshape(HT, cap, col_tiles, TW, 3, head_count, group_width).transpose(
        0, 2, 5, 1, 3, 4, 6
    )
    packed = jnp.roll(
        packed.reshape(seq_count * head_count, cap, TW, 3, group_width),
        -rotation * head_count,
        axis=0,
    )
    moved = lax.all_to_all(packed, ("seq", "head"), split_axis=0, concat_axis=0, tiled=True)
    band_lines = unpack_lines(moved, lines, cap, my_band, total_lines)
    tiles = band_lines.reshape(own_tiles, tile_size, 3, group_width)
    kv_part = tiles[:, :, 1:3, :]
    beside = [passed_along(kv_part, "seq", step) for step in (1, -1)]
    middle = jnp.stack([beside[0], kv_part, beside[1]])
    across = [passed_along(middle, "seq", step) for step in (col_tiles, -col_tiles)]
    widened = jnp.stack([across[0], middle, across[1]]).reshape(
        9 * own_tiles, tile_size, 2, group_width
    )
    usable = my_window >= 0
    safe = jnp.where(usable, my_window, my_block * own_tiles)
    owner = safe // own_tiles
    moment = safe % own_tiles
    delta_h = owner // col_tiles - my_band
    delta_w = owner % col_tiles - my_col
    local_ids = ((delta_h + 1) * 3 + delta_w + 1) * own_tiles + moment
    scale = HDIM ** (-0.5)

    def one_tile(args):
        query, picks, valid = args
        gathered = widened[picks].reshape(slot_count * tile_size, 2, group_width)
        usable_rows = jnp.repeat(valid, tile_size)
        outputs = []
        for head in range(head_local):
            low = head * HDIM
            outputs.append(
                head_attend(
                    query[:, low : low + HDIM],
                    gathered[:, 0, low : low + HDIM],
                    gathered[:, 1, low : low + HDIM],
                    usable_rows,
                    scale,
                )
            )
        return jnp.concatenate(outputs, axis=1)

    attended = lax.map(one_tile, (tiles[:, :, 0, :], local_ids, usable))
    band_out = attended.reshape(total_lines, TW, group_width)
    line_ids = start + jnp.arange(lines, dtype=jnp.int32)
    line_band = line_ids % (TH * HT) // TH
    line_slot = band_count(line_ids, line_band) - band_count(start, line_band)
    out_packed = pack_back(band_out, lines, cap, my_band, seq_count * head_count)
    back = lax.all_to_all(
        shortened(out_packed), ("seq", "head"), split_axis=0, concat_axis=0, tiled=True
    ).astype(out_packed.dtype)
    back = jnp.roll(back, rotation * head_count, axis=0)
    back = back.reshape(HT, col_tiles, head_count, cap, TW, group_width)
    got = back[line_band, :, :, line_slot]
    return got.transpose(0, 1, 3, 2, 4).reshape(rows, width)


def solution(mesh):
    in_specs = (P(("seq", "head"), None, None), P())
    out_specs = P(("seq", "head"), None)
    return jax.shard_map(body, mesh=mesh, in_specs=in_specs, out_specs=out_specs, check_vma=False)
```

profile of v0, /device:TPU:1, one launch (start us, length us, event | category | flops | bytes accessed | tf_op | source)
XLA Modules:
  0.0 633.3 jit_solution(16486938962675951900)
XLA Ops:
  0.0 0.1 compare_select_fusion.2
  0.1 0.1 fusion.41
  0.2 0.1 reshape.918
  0.3 1.2 copy-done
  1.5 4.5 gather_fusion.1
  6.0 4.7 copy.26
  10.7 3.6 select_bitcast_fusion
  14.4 4.3 copy.19
  18.7 3.2 slice.74
  21.9 0.1 slice.75
  22.0 6.5 %pad_maximum_fusion.1 = bf16[128,3,8,3,384]{4,2,3,1,0:T(8,128)(2,1)} fusion(bf16[16,3,8,3,384]{4,2,3,1,0:T(8,128)(2,1)S(1)} %slice.75, bf16[112,3,8,3,384]{4,2,3,1,0:T(8,128)(2,1)} %slice.74), kind=kLoop, calls=%fused_computation.45 | loop fusion | flops 3538944 | bytes 14155776 | tf_op jit(solution)/shard_map/jit(_roll_static)/concatenate | solution.py:106
  28.5 11.9 %all-to-all-start = ((bf16[128,3,8,3,384]{4,2,3,1,0:T(8,128)(2,1)}), bf16[128,3,8,3,384]{4,2,3,1,0:T(8,128)(2,1)}, u32[]{:S(2)}, u32[]{:S(2)}) async-start(bf16[128,3,8,3,384]{4,2,3,1,0:T(8,128)(2,1)} %pad_maximum_fusion.1), calls=%async_computation | async-start | bytes 14155776 | tf_op jit(solution)/shard_map/all_to_all | solution.py:111
  40.4 85.9 %all-to-all-done = bf16[128,3,8,3,384]{4,2,3,1,0:T(8,128)(2,1)} async-done(((bf16[128,3,8,3,384]{4,2,3,1,0:T(8,128)(2,1)}), bf16[128,3,8,3,384]{4,2,3,1,0:T(8,128)(2,1)}, u32[]{:S(2)}, u32[]{:S(2)}) %all-to-all-start) | async-done | bytes 7077920 | tf_op jit(solution)/shard_map/all_to_all | solution.py:111
  126.3 4.1 gather_fusion.2
  130.4 0.2 copy.20
  130.6 0.2 slice_bitcast_fusion.19
  130.8 0.1 collective-permute-start
  130.9 4.8 collective-permute-start.1
  135.7 24.8 %collective-permute-done = bf16[2,384,2,384]{3,1,0,2:T(8,128)(2,1)S(1)} collective-permute-done((bf16[2,384,2,384]{3,1,0,2:T(8,128)(2,1)S(1)}, bf16[2,384,2,384]{3,1,0,2:T(8,128)(2,1)S(1)}, u32[]{:S(2)}, u32[]{:S(2)}) %collective-permute-start) | collective-permute-done | bytes 1179680 | tf_op jit(solution)/shard_map/ppermute | solution.py:16
  160.5 3.1 fusion.63
  163.7 2.7 collective-permute-start.3
  166.3 0.1 compare_select_fusion.1
  166.5 0.2 reshape.934
  166.7 0.7 copy.18
  167.5 0.7 fusion.45
  168.2 0.6 pad_clamp_fusion.1
  168.8 72.3 %collective-permute-done.2 = bf16[3,2,384,2,384]{4,2,1,3,0:T(8,128)(2,1)} collective-permute-done((bf16[3,2,384,2,384]{4,2,1,3,0:T(8,128)(2,1)}, bf16[3,2,384,2,384]{4,2,1,3,0:T(8,128)(2,1)}, u32[]{:S(2)}, u32[]{:S(2)}) %collective-permute-start.2) | collective-permute-done | bytes 3538976 | tf_op jit(solution)/shard_map/ppermute | solution.py:16
  241.1 5.8 pad_maximum_fusion
  246.9 2.2 copy.21
  249.1 34.3 %copy.22 = bf16[18,384,2,384]{3,2,1,0:T(2,128)(2,1)} copy(bf16[18,384,2,384]{3,1,2,0:T(8,128)(2,1)S(1)} %bitcast.114) | data formatting | bytes 21233664 | tf_op jit(solution)/shard_map/while | solution.py:148
  283.4 290.5 %while.10 = (s32[]{:T(128)}, bf16[2,384,384]{2,1,0:T(8,128)(2,1)S(1)}, pred[2,27]{1,0:T(4,128)(4,1)S(1)}, bf16[2,384,384]{2,1,0:T(8,128)(2,1)S(1)}, s32[2,27]{1,...) while((s32[]{:T(128)}, bf16[2,384,384]{2,1,0:T(8,128)(2,1)S(1)}, pred[2,27]{1,0:T(4,128)(4,1)S(1)}, ...), condition=%wide.region_7.8_spmd, body=%wide.region_0.7_spmd.sunk | while | flops 6211877376 | bytes 225995248 | solution.py:148
  303.5 38.3 %gather_fusion = bf16[27,384,2,384]{3,2,1,0:T(2,128)(2,1)} fusion(bf16[18,384,2,384]{3,2,1,0:T(2,128)(2,1)} %get-tuple-element.146, s32[1024]{0:T(1024)S(1)} %pad_clamp_fusion.5), kind=kCustom, calls=%fused_computation.clone.1 | custom fusion | bytes 31850604 | tf_op jit(solution)/shard_map/while/body/eval_jaxpr/gather | solution.py:132
  341.8 14.7 %copy.29 = bf16[27,384,2,384]{3,1,0,2:T(8,128)(2,1)} copy(bf16[27,384,2,384]{3,2,1,0:T(2,128)(2,1)} %gather_fusion) | data formatting | bytes 31850496 | tf_op jit(solution)/shard_map/while/body/eval_jaxpr/gather | solution.py:132
  356.5 0.1 broadcast_in_dim.100
  356.6 9.8 %fusion.84 = (f32[384]{0:T(512)S(1)}, f32[384,10368]{1,0:T(8,128)}) fusion(bf16[10368,2,384]{2,0,1:T(8,128)(2,1)} %bitcast.108, bf16[384,384]{1,0:T(8,128)(2,1)S(1)} %dynamic-slice_bitcast_fusion.4, pred[10368]{0:T(1024)(128)(4,1)S(1)} %broadcast_in_dim.101), kind=kOutput, calls=%fused_computation.176.clone.1 | convolution fusion | flops 1031159424 | bytes 18690560 | tf_op jit(solution)/shard_map/while/body/eval_jaxpr/dot_general | solution.py:69
  366.4 7.8 %fusion.85 = f32[384]{0:T(512)S(1)} fusion(f32[384,10368]{1,0:T(8,128)} %get-tuple-element.125, f32[384]{0:T(512)S(1)} %get-tuple-element.126), kind=kLoop, calls=%fused_computation.17.clone.1 | loop fusion | flops 7962240 | bytes 15928320 | tf_op jit(solution)/shard_map/while/body/eval_jaxpr/reduce_sum | solution.py:75
  374.2 9.6 %fusion.86 = bf16[384,128]{0,1:T(8,128)(2,1)S(1)} fusion(bf16[10368,2,384]{2,0,1:T(8,128)(2,1)} %bitcast.109, f32[384,10368]{1,0:T(8,128)} %get-tuple-element.125, f32[384]{0:T(512)S(1)} %fusion.85, f32[384]{0:T(512)S(1)} %get-tuple-element.126), kind=kOutput, calls=%fused_computation.31.clone.1 | convolution fusion | flops 1031208960 | bytes 18680832 | tf_op jit(solution)/shard_map/while/body/eval_jaxpr/dot_general | solution.py:76
  383.8 9.8 %fusion.81 = (f32[384]{0:T(512)S(1)}, f32[384,10368]{1,0:T(8,128)}) fusion(bf16[10368,2,384]{2,0,1:T(8,128)(2,1)} %bitcast.110, bf16[384,384]{1,0:T(8,128)(2,1)S(1)} %dynamic-slice_bitcast_fusion.4, pred[10368]{0:T(1024)(128)(4,1)S(1)} %broadcast_in_dim.101), kind=kOutput, calls=%fused_computation.175.clone.1 | convolution fusion | flops 1031159424 | bytes 18690560 | tf_op jit(solution)/shard_map/while/body/eval_jaxpr/dot_general | solution.py:69
  393.6 7.8 %fusion.82 = f32[384]{0:T(512)S(1)} fusion(f32[384,10368]{1,0:T(8,128)} %get-tuple-element.123, f32[384]{0:T(512)S(1)} %get-tuple-element.124), kind=kLoop, calls=%fused_computation.18.clone.1 | loop fusion | flops 7962240 | bytes 15928320 | tf_op jit(solution)/shard_map/while/body/eval_jaxpr/reduce_sum | solution.py:75
  401.3 9.6 %fusion.83 = bf16[384,128]{0,1:T(8,128)(2,1)S(1)} fusion(bf16[10368,2,384]{2,0,1:T(8,128)(2,1)} %bitcast.111, f32[384,10368]{1,0:T(8,128)} %get-tuple-element.123, f32[384]{0:T(512)S(1)} %fusion.82, f32[384]{0:T(512)S(1)} %get-tuple-element.124), kind=kOutput, calls=%fused_computation.30.clone.1 | convolution fusion | flops 1031208960 | bytes 18680832 | tf_op jit(solution)/shard_map/while/body/eval_jaxpr/dot_general | solution.py:76
  410.9 9.8 %fusion.78 = (f32[384]{0:T(512)S(1)}, f32[384,10368]{1,0:T(8,128)}) fusion(bf16[10368,2,384]{2,0,1:T(8,128)(2,1)} %bitcast.112, bf16[384,384]{1,0:T(8,128)(2,1)S(1)} %dynamic-slice_bitcast_fusion.4, pred[10368]{0:T(1024)(128)(4,1)S(1)} %broadcast_in_dim.101), kind=kOutput, calls=%fused_computation.174.clone.1 | convolution fusion | flops 1031159424 | bytes 18690560 | tf_op jit(solution)/shard_map/while/body/eval_jaxpr/dot_general | solution.py:69
  420.7 7.8 %fusion.79 = f32[384]{0:T(512)S(1)} fusion(f32[384,10368]{1,0:T(8,128)} %get-tuple-element.121, f32[384]{0:T(512)S(1)} %get-tuple-element.122), kind=kLoop, calls=%fused_computation.19.clone.1 | loop fusion | flops 7962240 | bytes 15928320 | tf_op jit(solution)/shard_map/while/body/eval_jaxpr/reduce_sum | solution.py:75
  428.5 9.6 %fusion.80 = bf16[384,128]{0,1:T(8,128)(2,1)S(1)} fusion(bf16[10368,2,384]{2,0,1:T(8,128)(2,1)} %bitcast.113, f32[384,10368]{1,0:T(8,128)} %get-tuple-element.121, f32[384]{0:T(512)S(1)} %fusion.79, f32[384]{0:T(512)S(1)} %get-tuple-element.122), kind=kOutput, calls=%fused_computation.29.clone.1 | convolution fusion | flops 1031208960 | bytes 18680832 | tf_op jit(solution)/shard_map/while/body/eval_jaxpr/dot_general | solution.py:76
  438.1 0.2 copy.30
  438.5 38.7 %gather_fusion = bf16[27,384,2,384]{3,2,1,0:T(2,128)(2,1)} fusion(bf16[18,384,2,384]{3,2,1,0:T(2,128)(2,1)} %get-tuple-element.146, s32[1024]{0:T(1024)S(1)} %pad_clamp_fusion.5), kind=kCustom, calls=%fused_computation.clone.1 | custom fusion | bytes 31850604 | tf_op jit(solution)/shard_map/while/body/eval_jaxpr/gather | solution.py:132
  477.2 14.7 %copy.29 = bf16[27,384,2,384]{3,1,0,2:T(8,128)(2,1)} copy(bf16[27,384,2,384]{3,2,1,0:T(2,128)(2,1)} %gather_fusion) | data formatting | bytes 31850496 | tf_op jit(solution)/shard_map/while/body/eval_jaxpr/gather | solution.py:132
  492.0 9.8 %fusion.84 = (f32[384]{0:T(512)S(1)}, f32[384,10368]{1,0:T(8,128)}) fusion(bf16[10368,2,384]{2,0,1:T(8,128)(2,1)} %bitcast.108, bf16[384,384]{1,0:T(8,128)(2,1)S(1)} %dynamic-slice_bitcast_fusion.4, pred[10368]{0:T(1024)(128)(4,1)S(1)} %broadcast_in_dim.101), kind=kOutput, calls=%fused_computation.176.clone.1 | convolution fusion | flops 1031159424 | bytes 18690560 | tf_op jit(solution)/shard_map/while/body/eval_jaxpr/dot_general | solution.py:69
  501.8 7.8 %fusion.85 = f32[384]{0:T(512)S(1)} fusion(f32[384,10368]{1,0:T(8,128)} %get-tuple-element.125, f32[384]{0:T(512)S(1)} %get-tuple-element.126), kind=kLoop, calls=%fused_computation.17.clone.1 | loop fusion | flops 7962240 | bytes 15928320 | tf_op jit(solution)/shard_map/while/body/eval_jaxpr/reduce_sum | solution.py:75
  509.6 9.6 %fusion.86 = bf16[384,128]{0,1:T(8,128)(2,1)S(1)} fusion(bf16[10368,2,384]{2,0,1:T(8,128)(2,1)} %bitcast.109, f32[384,10368]{1,0:T(8,128)} %get-tuple-element.125, f32[384]{0:T(512)S(1)} %fusion.85, f32[384]{0:T(512)S(1)} %get-tuple-element.126), kind=kOutput, calls=%fused_computation.31.clone.1 | convolution fusion | flops 1031208960 | bytes 18680832 | tf_op jit(solution)/shard_map/while/body/eval_jaxpr/dot_general | solution.py:76
  519.2 9.8 %fusion.81 = (f32[384]{0:T(512)S(1)}, f32[384,10368]{1,0:T(8,128)}) fusion(bf16[10368,2,384]{2,0,1:T(8,128)(2,1)} %bitcast.110, bf16[384,384]{1,0:T(8,128)(2,1)S(1)} %dynamic-slice_bitcast_fusion.4, pred[10368]{0:T(1024)(128)(4,1)S(1)} %broadcast_in_dim.101), kind=kOutput, calls=%fused_computation.175.clone.1 | convolution fusion | flops 1031159424 | bytes 18690560 | tf_op jit(solution)/shard_map/while/body/eval_jaxpr/dot_general | solution.py:69
  529.0 7.8 %fusion.82 = f32[384]{0:T(512)S(1)} fusion(f32[384,10368]{1,0:T(8,128)} %get-tuple-element.123, f32[384]{0:T(512)S(1)} %get-tuple-element.124), kind=kLoop, calls=%fused_computation.18.clone.1 | loop fusion | flops 7962240 | bytes 15928320 | tf_op jit(solution)/shard_map/while/body/eval_jaxpr/reduce_sum | solution.py:75
  536.8 9.6 %fusion.83 = bf16[384,128]{0,1:T(8,128)(2,1)S(1)} fusion(bf16[10368,2,384]{2,0,1:T(8,128)(2,1)} %bitcast.111, f32[384,10368]{1,0:T(8,128)} %get-tuple-element.123, f32[384]{0:T(512)S(1)} %fusion.82, f32[384]{0:T(512)S(1)} %get-tuple-element.124), kind=kOutput, calls=%fused_computation.30.clone.1 | convolution fusion | flops 1031208960 | bytes 18680832 | tf_op jit(solution)/shard_map/while/body/eval_jaxpr/dot_general | solution.py:76
  546.4 9.8 %fusion.78 = (f32[384]{0:T(512)S(1)}, f32[384,10368]{1,0:T(8,128)}) fusion(bf16[10368,2,384]{2,0,1:T(8,128)(2,1)} %bitcast.112, bf16[384,384]{1,0:T(8,128)(2,1)S(1)} %dynamic-slice_bitcast_fusion.4, pred[10368]{0:T(1024)(128)(4,1)S(1)} %broadcast_in_dim.101), kind=kOutput, calls=%fused_computation.174.clone.1 | convolution fusion | flops 1031159424 | bytes 18690560 | tf_op jit(solution)/shard_map/while/body/eval_jaxpr/dot_general | solution.py:69
  556.2 7.8 %fusion.79 = f32[384]{0:T(512)S(1)} fusion(f32[384,10368]{1,0:T(8,128)} %get-tuple-element.121, f32[384]{0:T(512)S(1)} %get-tuple-element.122), kind=kLoop, calls=%fused_computation.19.clone.1 | loop fusion | flops 7962240 | bytes 15928320 | tf_op jit(solution)/shard_map/while/body/eval_jaxpr/reduce_sum | solution.py:75
  563.9 9.6 %fusion.80 = bf16[384,128]{0,1:T(8,128)(2,1)S(1)} fusion(bf16[10368,2,384]{2,0,1:T(8,128)(2,1)} %bitcast.113, f32[384,10368]{1,0:T(8,128)} %get-tuple-element.121, f32[384]{0:T(512)S(1)} %fusion.79, f32[384]{0:T(512)S(1)} %get-tuple-element.122), kind=kOutput, calls=%fused_computation.29.clone.1 | convolution fusion | flops 1031208960 | bytes 18680832 | tf_op jit(solution)/shard_map/while/body/eval_jaxpr/dot_general | solution.py:76
  573.6 0.2 copy.30
  573.9 2.9 gather_fusion.3
  576.8 3.1 broadcast_select_fusion
  579.9 12.4 %all-to-all-start.1 = ((bf16[128,3,8,384]{3,2,1,0:T(8,128)(2,1)}), bf16[128,3,8,384]{3,2,1,0:T(8,128)(2,1)}, u32[]{:S(2)}, u32[]{:S(2)}) async-start(bf16[128,3,8,384]{3,2,1,0:T(8,128)(2,1)} %broadcast_select_fusion), calls=%async_computation.1 | async-start | bytes 4718592 | tf_op jit(solution)/shard_map/all_to_all | solution.py:154
  592.4 32.9 %all-to-all-done.1 = bf16[128,3,8,384]{3,2,1,0:T(8,128)(2,1)} async-done(((bf16[128,3,8,384]{3,2,1,0:T(8,128)(2,1)}), bf16[128,3,8,384]{3,2,1,0:T(8,128)(2,1)}, u32[]{:S(2)}, u32[]{:S(2)}) %all-to-all-start.1) | async-done | bytes 2359328 | tf_op jit(solution)/shard_map/all_to_all | solution.py:154
  625.3 1.8 slice.79
  627.1 1.0 slice.78
  628.1 1.7 pad_maximum_fusion.3
  629.7 3.1 gather_fusion.4
  (34 shorter events, 0.6 us)
Async XLA Ops:
  0.0 1.5 copy-start
  28.5 97.9 %all-to-all-start = ((bf16[128,3,8,3,384]{4,2,3,1,0:T(8,128)(2,1)}), bf16[128,3,8,3,384]{4,2,3,1,0:T(8,128)(2,1)}, u32[]{:S(2)}, u32[]{:S(2)}) async-start(bf16[128,3,8,3,384]{4,2,3,1,0:T(8,128)(2,1)} %pad_maximum_fusion.1), calls=%async_computation | async-start | bytes 14155776 | tf_op jit(solution)/shard_map/all_to_all | solution.py:111
  130.8 29.7 %collective-permute-start = (bf16[2,384,2,384]{3,1,0,2:T(8,128)(2,1)S(1)}, bf16[2,384,2,384]{3,1,0,2:T(8,128)(2,1)S(1)}, u32[]{:S(2)}, u32[]{:S(2)}) collective-permute-start(bf16[2,384,2,384]{3,1,0,2:T(8,128)(2,1)S(1)} %get-tuple-element.73), channel_id=1, source_target_pairs={{0,8},{8,16},{16,24},{24,32},{32,40},{40,48},{48,56},{56,64},{64,7... | collective-permute-start | bytes 3538952 | tf_op jit(solution)/shard_map/ppermute | solution.py:16
  130.9 29.6 %collective-permute-start.1 = (bf16[2,384,2,384]{3,1,0,2:T(8,128)(2,1)S(1)}, bf16[2,384,2,384]{3,1,0,2:T(8,128)(2,1)S(1)}, u32[]{:S(2)}, u32[]{:S(2)}) collective-permute-start(bf16[2,384,2,384]{3,1,0,2:T(8,128)(2,1)S(1)} %get-tuple-element.73), channel_id=1, source_target_pairs={{0,120},{8,0},{16,8},{24,16},{32,24},{40,32},{48,40},{56,48},{64,5... | collective-permute-start | bytes 3538952 | tf_op jit(solution)/shard_map/ppermute | solution.py:16
  163.7 77.5 %collective-permute-start.2 = (bf16[3,2,384,2,384]{4,2,1,3,0:T(8,128)(2,1)}, bf16[3,2,384,2,384]{4,2,1,3,0:T(8,128)(2,1)}, u32[]{:S(2)}, u32[]{:S(2)}) collective-permute-start(bf16[3,2,384,2,384]{4,2,1,3,0:T(8,128)(2,1)} %get-tuple-element.71), channel_id=1, source_target_pairs={{0,32},{8,40},{16,48},{24,56},{32,64},{40,72},{48,80},{56,88},{64,... | collective-permute-start | bytes 10616840 | tf_op jit(solution)/shard_map/ppermute | solution.py:16
  163.7 77.5 %collective-permute-start.3 = (bf16[3,2,384,2,384]{4,2,1,3,0:T(8,128)(2,1)}, bf16[3,2,384,2,384]{4,2,1,3,0:T(8,128)(2,1)}, u32[]{:S(2)}, u32[]{:S(2)}) collective-permute-start(bf16[3,2,384,2,384]{4,2,1,3,0:T(8,128)(2,1)} %get-tuple-element.71), channel_id=1, source_target_pairs={{0,96},{8,104},{16,112},{24,120},{32,0},{40,8},{48,16},{56,24},{64... | collective-permute-start | bytes 10616840 | tf_op jit(solution)/shard_map/ppermute | solution.py:16
  283.4 290.5 %copy-start.2 = (s32[1024]{0:T(1024)S(1)}, s32[1024]{0:T(1024)}, u32[]{:S(2)}) copy-start(s32[1024]{0:T(1024)} %pad_clamp_fusion.1) | copy-start | bytes 12292
  283.4 293.4 %copy-start.3 = (pred[128,3]{1,0:T(8,128)(4,1)S(1)}, pred[128,3]{1,0:T(8,128)(4,1)}, u32[]{:S(2)}) copy-start(pred[128,3]{1,0:T(8,128)(4,1)} %copy.18) | copy-start | bytes 1156
  576.8 56.1 %copy-start.1 = (bf16[96,3,3072]{2,0,1:T(8,128)(2,1)S(1)}, bf16[96,3,3072]{2,0,1:T(8,128)(2,1)}, u32[]{:S(2)}) copy-start(bf16[96,3,3072]{2,0,1:T(8,128)(2,1)} %param.4) | copy-start | bytes 5308420
  579.9 45.4 %all-to-all-start.1 = ((bf16[128,3,8,384]{3,2,1,0:T(8,128)(2,1)}), bf16[128,3,8,384]{3,2,1,0:T(8,128)(2,1)}, u32[]{:S(2)}, u32[]{:S(2)}) async-start(bf16[128,3,8,384]{3,2,1,0:T(8,128)(2,1)} %broadcast_select_fusion), calls=%async_computation.1 | async-start | bytes 4718592 | tf_op jit(solution)/shard_map/all_to_all | solution.py:154
where the time goes:
time: 643 us; the launch traced here: 633 us
  waiting for transfers between devices  216 us (34%)
  local copies, waits for them, and re-layouts  176 us (27%)
  matrix products  116 us (18%)
  other arithmetic  72.3 us (11%)
  starting transfers between devices  31.8 us (5%)
  loops' own time  20.2 us (3%)
    gather x4, local copies, waits for them, and re-layouts, one_tile(): gathered = widened[picks].reshape(slot_count * tile_size, 2, group_width)  106 us
    ppermute x4, waiting for transfers between devices, passed_along(): return lax.ppermute(value, axis, pairs)  97.1 us
    all_to_all x1, waiting for transfers between devices, body(): lax.all_to_all(packed, ('seq', 'head'), split_axis=0, concat_axis=0, tile...  85.9 us
    dot_general x6, matrix products, head_attend(): lax.dot_general(query, keys, (((1,), (1,)), ((), ())), preferred_element_...  58.7 us
    dot_general x6, matrix products, head_attend(): jnp.dot(weights, values, preferred_element_type=jnp.float32)  57.6 us
    reduce_sum x6, other arithmetic, head_attend(): weights = (expo / jnp.sum(expo, axis=1, keepdims=True)).astype(jnp.bfloat16)  46.6 us
    while x1, local copies, waits for them, and re-layouts, body(): attended = lax.map(one_tile, (tiles[:, :, 0, :], local_ids, usable))  34.3 us
    all_to_all x1, waiting for transfers between devices, body(): lax.all_to_all(shortened(out_packed), ('seq', 'head'), split_axis=0, conc...  32.9 us
  transfers between devices with their start and end apart: 6, of which 4 were waited for; matrix products, arithmetic and copies ran while one was open for 0% of the time, Pallas kernels for 0%

commit v1 on v0

v1 whole, which is shorter than its diff:
```python
import jax
import jax.numpy as jnp
from jax import lax
from jax.experimental import pallas as pl
from jax.experimental.pallas import tpu as pltpu
from jax.sharding import PartitionSpec as P

HEADS = 24
HDIM = 128
TF = 6
TH = 8
TW = 8
HT = 4
WT = 4
TILE = TF * TH * TW
LINES = 3
ROWS = LINES * TW
PEERS = 64
OWNERS = 48
KCOLS = 3
QCOLS = 2
SLOTS = 27
MESH = pl.DeviceIdType.MESH
SCALE = HDIM**-0.5
LOG2E = 1.4426950408889634


def place():
    seq = lax.axis_index("seq")
    head = lax.axis_index("head")
    rank = lax.rem(head // 2 + seq // 4 + lax.rem(seq, 4), 4)
    return seq, head, rank, lax.rem(head, 2)


def bring(packed, queries, keyvals, send_q, recv_q, send_kv, recv_kv, send_x, recv_x):
    seq, head, rank, core = place()
    time = seq // 8
    mine = lax.rem(seq, 8) * 8 + head
    owner = rank < 3
    to_self = owner & (core == time)

    def copies(step):
        there = lax.rem(seq + step, 16)
        row = lax.rem(step // 16 + seq, 3)
        half = lax.rem(there, 2)
        which = row * 8 + there // 2
        chip = lax.rem(row + 8 - there // 4 - lax.rem(there, 4), 4)
        target = chip * 2 + time
        pairs = (
            (packed.at[0, pl.ds(2 * half, QCOLS), which], queries.at[:, mine], send_q, recv_q),
            (packed.at[pl.ds(1, 2), pl.ds(half, KCOLS), which], keyvals.at[time, :, :, mine], send_kv, recv_kv),
        )
        return there, target, pairs

    def start(step, carry):
        there, target, pairs = copies(step)
        own = (there == seq) & (target == head)

        @pl.when(own)
        def _():
            for source, landing, _, arrived in pairs:
                pltpu.make_async_copy(source, landing, arrived).start()

        @pl.when(jnp.logical_not(own))
        def _():
            for source, landing, sent, arrived in pairs:
                pltpu.make_async_remote_copy(
                    src_ref=source,
                    dst_ref=landing,
                    send_sem=sent,
                    recv_sem=arrived,
                    device_id=(there, target),
                    device_id_type=MESH,
                ).start()

        return carry

    lax.fori_loop(0, OWNERS, start, 0)

    @pl.when(owner)
    def _():
        pltpu.make_async_copy(keyvals.at[core], keyvals.at[core], recv_kv).wait()
        swap = pltpu.make_async_remote_copy(
            src_ref=keyvals.at[core],
            dst_ref=keyvals.at[core],
            send_sem=send_x,
            recv_sem=recv_x,
            device_id=(seq, head + 1 - 2 * core),
            device_id_type=MESH,
        )
        swap.start()
        pltpu.make_async_copy(queries, queries, recv_q).wait()
        swap.wait_send()
        pltpu.make_async_copy(keyvals.at[1 - core], keyvals.at[1 - core], recv_x).wait()

    def sent(count):
        spread = keyvals.at[0, :, :, pl.ds(0, count)]
        pltpu.make_async_copy(spread, spread, send_kv).wait()
        spread = queries.at[:, pl.ds(0, count)]
        pltpu.make_async_copy(spread, spread, send_q).wait()

    @pl.when(to_self)
    def _():
        sent(OWNERS - 1)

    @pl.when(jnp.logical_not(to_self))
    def _():
        sent(OWNERS)


def attend(meta, table, q_ref, kv_ref, o_ref, top, total, acc):
    column, band = pl.program_id(0), pl.program_id(1)
    half, time, owner = meta[0], meta[1], meta[2]
    here = (band * WT + 2 * half + column) * 2 + time

    @pl.when(owner == 1)
    def _():
        query = q_ref[0, :, 0].reshape(TILE, HDIM)
        top[...] = jnp.full_like(top, -jnp.inf)
        total[...] = jnp.zeros_like(total)
        acc[...] = jnp.zeros_like(acc)

        def slot(index, carry):
            pick = table[here, index]

            @pl.when(pick >= 0)
            def _():
                moment = lax.rem(pick, 2)
                across = lax.rem(pick // 2, WT) - half
                down = pick // (2 * WT)
                keys = kv_ref[moment, 0, across, :, down].reshape(TILE, HDIM)
                values = kv_ref[moment, 1, across, :, down].reshape(TILE, HDIM)
                scores = lax.dot_general(query, keys, (((1,), (1,)), ((), ())), preferred_element_type=jnp.float32)
                before = top[...]
                peak = jnp.maximum(before, jnp.max(scores, axis=1, keepdims=True))
                top[...] = peak
                fade = jnp.exp2((before - peak) * (SCALE * LOG2E))
                expo = jnp.exp2((scores - peak[:, :1]) * (SCALE * LOG2E))
                lanes = expo[:, :HDIM] + expo[:, HDIM : 2 * HDIM] + expo[:, 2 * HDIM :]
                total[...] = total[...] * fade + lanes
                acc[...] = acc[...] * fade + jnp.dot(
                    expo.astype(jnp.bfloat16), values, preferred_element_type=jnp.float32
                )

            return carry

        lax.fori_loop(0, SLOTS, slot, 0)
        denominator = jnp.sum(total[...], axis=1, keepdims=True)
        o_ref[0, :, 0] = (acc[...] / denominator).astype(jnp.bfloat16).reshape(TF, TH * TW, HDIM)


def give(answers, stage, send, recv):
    seq, head, rank, core = place()
    owner = rank < 3
    to_self = owner & (core == seq // 8)
    which = rank * 8 + seq // 2
    half = lax.rem(seq, 2)

    @pl.when(owner)
    def _():
        def start(step, carry):
            number = lax.rem(step + lax.rem(seq, 8) * 8 + head, PEERS)
            there = core * 8 + number // 8
            target = lax.rem(number, 8)
            source = answers.at[:, number]
            landing = stage.at[pl.ds(2 * half, QCOLS), which]
            own = (there == seq) & (target == head)

            @pl.when(own)
            def _():
                pltpu.make_async_copy(source, landing, recv).start()

            @pl.when(jnp.logical_not(own))
            def _():
                pltpu.make_async_remote_copy(
                    src_ref=source,
                    dst_ref=landing,
                    send_sem=send,
                    recv_sem=recv,
                    device_id=(there, target),
                    device_id_type=MESH,
                ).start()

            return carry

        lax.fori_loop(0, PEERS, start, 0)

    pltpu.make_async_copy(stage, stage, recv).wait()

    def sent(count):
        spread = answers.at[:, pl.ds(0, count)]
        pltpu.make_async_copy(spread, spread, send).wait()

    @pl.when(to_self)
    def _():
        sent(PEERS - 1)

    @pl.when(owner & jnp.logical_not(to_self))
    def _():
        sent(PEERS)


def body(qkv, window_tiles):
    seq, _, rank, core = place()
    anywhere = pl.BlockSpec(memory_space=pl.ANY)
    packed = qkv.reshape(LINES, WT, TW, 3, HEADS, HDIM).transpose(3, 1, 4, 0, 2, 5).reshape(3, WT, HEADS, ROWS, HDIM)
    queries, keyvals = pl.pallas_call(
        bring,
        out_shape=(
            jax.ShapeDtypeStruct((QCOLS, PEERS, ROWS, HDIM), jnp.bfloat16),
            jax.ShapeDtypeStruct((2, 2, KCOLS, PEERS, ROWS, HDIM), jnp.bfloat16),
        ),
        in_specs=[anywhere],
        out_specs=(anywhere, anywhere),
        scratch_shapes=[pltpu.SemaphoreType.DMA] * 6,
        compiler_params=pltpu.CompilerParams(has_side_effects=True),
        name="bring",
    )(packed)
    meta = jnp.stack([lax.rem(seq, 2), core, (rank < 3).astype(jnp.int32)])
    answers = pl.pallas_call(
        attend,
        out_shape=jax.ShapeDtypeStruct((QCOLS, TF, HT, TH * TW, HDIM), jnp.bfloat16),
        grid_spec=pltpu.PrefetchScalarGridSpec(
            num_scalar_prefetch=2,
            grid=(QCOLS, HT),
            in_specs=[
                pl.BlockSpec((1, TF, 1, TH * TW, HDIM), lambda i, j, *_: (i, 0, j, 0, 0)),
                pl.BlockSpec(memory_space=pltpu.VMEM),
            ],
            out_specs=pl.BlockSpec((1, TF, 1, TH * TW, HDIM), lambda i, j, *_: (i, 0, j, 0, 0)),
            scratch_shapes=[pltpu.VMEM((TILE, HDIM), jnp.float32)] * 3,
        ),
        compiler_params=pltpu.CompilerParams(vmem_limit_bytes=40 << 20),
        name="attend",
    )(
        meta,
        window_tiles,
        queries.reshape(QCOLS, TF, HT, TH * TW, HDIM),
        keyvals.reshape(2, 2, KCOLS, TF, HT, TH * TW, HDIM),
    )
    stage = pl.pallas_call(
        give,
        out_shape=jax.ShapeDtypeStruct((WT, HEADS, ROWS, HDIM), jnp.bfloat16),
        in_specs=[anywhere],
        out_specs=anywhere,
        scratch_shapes=[pltpu.SemaphoreType.DMA] * 2,
        compiler_params=pltpu.CompilerParams(has_side_effects=True),
        name="give",
    )(answers.reshape(QCOLS, PEERS, ROWS, HDIM))
    return stage.reshape(WT, HEADS, LINES, TW, HDIM).transpose(2, 0, 3, 1, 4).reshape(LINES * WT * TW, HEADS * HDIM)


def solution(mesh):
    in_specs = (P(("seq", "head"), None, None), P())
    out_specs = P(("seq", "head"), None)
    return jax.shard_map(body, mesh=mesh, in_specs=in_specs, out_specs=out_specs, check_vma=False)
```

time: 643 us -> 154 us (0.24); the launches traced: 633 us -> 153 us
  waiting for transfers between devices: 216 us -> 0 us
  local copies, waits for them, and re-layouts: 176 us -> 9.41 us
  Pallas kernels: 0 us -> 144 us
  matrix products: 116 us -> 0 us
  other arithmetic: 72.3 us -> 0.08 us
  starting transfers between devices: 31.8 us -> 0 us
  loops' own time: 20.2 us -> 0 us
    pallas_call x0 -> x3, Pallas kernels: none -> 144 us  [the longest x1 56.7 us: body(): pl.pallas_call(attend, out_shape=jax.ShapeDtypeStruct((QCOLS, TF, HT, TH...]
    gather x9 -> x0, local copies, waits for them, and re-layouts: 121 us -> none  [the longest x4 106 us: one_tile(): gathered = widened[picks].reshape(slot_count * tile_size, 2, group_width)]
    all_to_all x2 -> x0, waiting for transfers between devices: 119 us -> none  [the longest x1 85.9 us: body(): lax.all_to_all(packed, ('seq', 'head'), split_axis=0, concat_axis=0, tile...]
    dot_general x12 -> x0, matrix products: 116 us -> none  [the longest x6 58.7 us: head_attend(): lax.dot_general(query, keys, (((1,), (1,)), ((), ())), preferred_element_...]
    ppermute x4 -> x0, waiting for transfers between devices: 97.1 us -> none  [passed_along(): return lax.ppermute(value, axis, pairs)]
    reduce_sum x6 -> x0, other arithmetic: 46.6 us -> none  [head_attend(): weights = (expo / jnp.sum(expo, axis=1, keepdims=True)).astype(jnp.bfloat16)]
    while x1 -> x0, local copies, waits for them, and re-layouts: 34.3 us -> none  [body(): attended = lax.map(one_tile, (tiles[:, :, 0, :], local_ids, usable))]
    all_to_all x2 -> x0, starting transfers between devices: 24.3 us -> none  [the longest x1 12.4 us: body(): lax.all_to_all(shortened(out_packed), ('seq', 'head'), split_axis=0, conc...]
  transfers between devices with their start and end apart: 6 -> 0, of which waited for: 4 -> 0; matrix products, arithmetic and copies ran while one was open for 0% -> 0% of each run, Pallas kernels for 0% -> 0%
where the time goes in v1:
time: 154 us; the launch traced here: 153 us
  Pallas kernels  144 us (94%)
  local copies, waits for them, and re-layouts  9.41 us (6%)
    pallas_call x1, Pallas kernels, body(): pl.pallas_call(attend, out_shape=jax.ShapeDtypeStruct((QCOLS, TF, HT, TH...  56.7 us
    pallas_call x1, Pallas kernels, body(): pl.pallas_call(bring, out_shape=(jax.ShapeDtypeStruct((QCOLS, PEERS, ROWS...  56.1 us
    pallas_call x1, Pallas kernels, body(): pl.pallas_call(give, out_shape=jax.ShapeDtypeStruct((WT, HEADS, ROWS, HDI...  31 us
    unnamed x8, local copies, waits for them, and re-layouts  4.35 us

profile of v1, /device:TPU:1, one launch (start us, length us, event | category | flops | bytes accessed | tf_op | source)
XLA Modules:
  0.0 153.4 jit_solution(1586541271893740477)
XLA Ops:
  0.0 0.1 pad_add_fusion.meta
  0.1 3.0 %copy.6 = bf16[3,4,8,3,24,128]{5,2,0,4,1,3:T(8,128)(2,1)} copy(bf16[3,4,8,3,24,128]{5,2,4,1,0,3:T(8,128)(2,1)} %bitcast.21) | data formatting | bytes 3538944 | tf_op jit(solution)/shard_map/reshape | solution.py:206
  3.1 0.0 copy-start.3
  3.1 56.1 %bring.1 = (bf16[2,64,24,128]{3,2,1,0:T(8,128)(2,1)}, bf16[2,2,3,64,24,128]{5,4,3,2,1,0:T(8,128)(2,1)}) custom-call(bf16[3,4,24,24,128]{4,3,2,1,0:T(8,128)(2,1)} %bitcast.19), custom_call_target="tpu_custom_call" | custom-call | tf_op jit(solution)/shard_map/bring/pallas_call | solution.py:207
  59.3 0.0 copy-done.3
  59.3 0.0 copy-start
  59.3 2.3 %copy-done = bf16[2,2,3,64,24,128]{5,4,3,2,1,0:T(8,128)(2,1)S(1)} copy-done((bf16[2,2,3,64,24,128]{5,4,3,2,1,0:T(8,128)(2,1)S(1)}, bf16[2,2,3,64,24,128]{5,4,3,2,1,0:T(8,128)(2,1)}, u32[]{:S(2)}) %copy-start) | copy-done | bytes 4718616
  61.6 0.0 copy-start.2
  61.6 1.1 copy-done.2
  62.8 56.7 %attend.1 = bf16[2,6,4,64,128]{4,3,2,1,0:T(8,128)(2,1)S(1)} custom-call(s32[3]{0:T(128)S(1)} %pad_add_fusion.meta, s32[32,27]{1,0:T(8,128)S(1)} %copy-done.3, bf16[2,6,4,64,128]{4,3,2,1,0:T(8,128)(2,1)S(1)} %bitcast.18, bf16[2,2,3,6,4,64,128]{6,5,4,3,2,1,0:T(8,128)(2,1)S(1)} %bitcast.16), custom_call_target="tpu_custom_call" | custom-call | tf_op jit(solution)/shard_map/attend/pallas_call | solution.py:220
  119.5 0.0 copy-start.1
  119.5 0.9 copy-done.1
  120.4 31.0 %give.1 = bf16[4,24,24,128]{3,2,1,0:T(8,128)(2,1)} custom-call(bf16[2,64,24,128]{3,2,1,0:T(8,128)(2,1)} %bitcast.17), custom_call_target="tpu_custom_call" | custom-call | tf_op jit(solution)/shard_map/give/pallas_call | solution.py:241
  151.3 2.0 %copy.4 = bf16[3,4,8,24,128]{4,2,3,1,0:T(8,128)(2,1)} copy(bf16[3,4,8,24,128]{4,2,0,3,1:T(8,128)(2,1)} %bitcast.20) | data formatting | bytes 1179648 | tf_op jit(solution)/shard_map/transpose | solution.py:250
Async XLA Ops:
  3.1 56.2 %copy-start.3 = (s32[32,27]{1,0:T(8,128)S(1)}, s32[32,27]{1,0:T(8,128)}, u32[]{:S(2)}) copy-start(s32[32,27]{1,0:T(8,128)} %table.1) | copy-start | bytes 10372
  59.3 2.3 %copy-start = (bf16[2,2,3,64,24,128]{5,4,3,2,1,0:T(8,128)(2,1)S(1)}, bf16[2,2,3,64,24,128]{5,4,3,2,1,0:T(8,128)(2,1)}, u32[]{:S(2)}) copy-start(bf16[2,2,3,64,24,128]{5,4,3,2,1,0:T(8,128)(2,1)} %get-tuple-element.8) | copy-start | bytes 14155780
  61.6 1.1 copy-start.2
  119.5 0.9 copy-start.1
